TPU v7x, 256 devices: a whole 4x4x8 slice. The times are simulated.
256 devices in a mesh: row: 32 (over z_hi, x, core), col: 8 (over y, z_lo).
Axes of the slice: x: 4, y: 4, z: 8 (z_hi: 4, z_lo: 2; z = z_hi * 2 + z_lo), core: 2. Of those that a mesh axis runs over, the one named last changes fastest.
Arguments:
- amplitudes: bfloat16 [512, 640000], P(('row', 'col')), may hold values from -6 to 6
- integrals: bfloat16 [2, 800, 640000], P(None, None, ('row', 'col')), may hold values from -0.0078125 to 0.0078125
Outputs:
- ladder: float32 [512, 2, 800], P(('row', 'col'))
All inputs are finite; a program needn't handle non-finite values.
Results may differ from a plain program's by a relative error of at most 0.0003.
Values may be sent and summed in bfloat16 or wider, within the bound.
A program may use at most 64 MiB of HBM per device.

v0:
```python
import jax
import jax.numpy as jnp
from jax import lax
from jax.sharding import PartitionSpec as P


def shards(amplitudes, integrals):
    row_count = lax.axis_size("row")
    col_count = lax.axis_size("col")
    pair_local = amplitudes.shape[0]
    full_width = amplitudes.shape[1]
    slab_width = full_width // (row_count * col_count)
    sectioned = amplitudes.reshape(1, 1, pair_local, row_count, col_count, slab_width)
    remapped = lax.all_to_all(
        lax.all_to_all(sectioned, "row", split_axis=3, concat_axis=0, tiled=True),
        "col",
        split_axis=4,
        concat_axis=1,
        tiled=True,
    )
    local_amps = remapped.reshape(row_count * col_count * pair_local, slab_width)
    window_size = integrals.shape[0]
    virtual_count = integrals.shape[1]
    flat_ints = integrals.reshape(window_size * virtual_count, slab_width)
    product = lax.dot_general(
        local_amps, flat_ints, (((1,), (1,)), ((), ())), preferred_element_type=jnp.float32
    )
    return lax.psum_scatter(
        product.reshape(local_amps.shape[0], window_size, virtual_count),
        ("row", "col"),
        scatter_dimension=0,
        tiled=True,
    )


def solution(mesh):
    return jax.shard_map(
        shards,
        mesh=mesh,
        in_specs=(P(("row", "col"), None), P(None, None, ("row", "col"))),
        out_specs=P(("row", "col"), None, None),
        check_vma=False,
    )
```

profile of v0, /device:TPU:3, one launch (start us, length us, event | category | flops | bytes accessed | tf_op | source)
XLA Modules:
  0.0 418.3 jit_solution(11135531921940909285)
XLA Ops:
  6.5 0.0 all-reduce.3.cloned.1.call-start
  6.5 4.8 %reshape.16 = bf16[1280000]{0:T(1024)(128)(2,1)} reshape(bf16[2,640000]{1,0:T(2,128)(2,1)} %param.2) | data formatting | bytes 5120000
  11.4 5.5 %reshape.11 = bf16[1,1,2,32,8,2500]{5,4,3,2,1,0:T(8,128)(2,1)S(1)} reshape(bf16[1280000]{0:T(1024)(128)(2,1)} %reshape.16) | data formatting | bytes 5120000 | tf_op jit(solution)/shard_map/reshape | solution.py:13
  16.9 2.7 copy.12
  19.6 72.8 %all_to_all.33 = bf16[1,1,2,32,8,2500]{5,2,4,1,0,3:T(2,128)(2,1)S(1)} all-to-all(bf16[1,1,2,32,8,2500]{5,2,4,1,0,3:T(2,128)(2,1)S(1)} %copy.12), channel_id=1, replica_groups=mesh['row'=32,'col'=8] {'row'}, dimensions={3} | all-to-all | bytes 5120000 | tf_op jit(solution)/shard_map/all_to_all | solution.py:15
  92.4 1.8 copy.13
  94.2 36.7 %all_to_all.34 = bf16[32,1,2,1,8,2500]{5,2,0,3,1,4:T(2,128)(2,1)S(1)} all-to-all(bf16[32,1,2,1,8,2500]{5,2,0,3,1,4:T(2,128)(2,1)S(1)} %copy.13), channel_id=1, replica_groups=mesh['row'=32,'col'=8] {'col'}, dimensions={4} | all-to-all | bytes 5120000 | tf_op jit(solution)/shard_map/all_to_all | solution.py:14
  130.9 2.7 copy.14
  133.7 3.2 reshape.12
  136.8 10.1 %fusion = f32[512,2,800]{2,0,1:T(8,128)} fusion(bf16[2,800,2500]{2,1,0:T(8,128)(2,1)} %param.3, bf16[512,2500]{1,0:T(8,128)(2,1)} %reshape.12), kind=kOutput, calls=%fused_computation | convolution fusion | flops 4096000000 | bytes 13836800 | tf_op jit(solution)/shard_map/dot_general | solution.py:25
  146.9 0.0 all-reduce.3.cloned.1.call-update
  147.0 263.1 %all-reduce.3.cloned.1.call-done = f32[512,2,800]{2,0,1:T(8,128)} async-done(((f32[512,2,800]{2,0,1:T(8,128)}), f32[512,2,800]{2,0,1:T(8,128)}) %all-reduce.3.cloned.1.call-update) | async-done | bytes 3276816
  410.0 0.8 constant_dynamic-slice_fusion
  410.9 0.6 copy.16
Async XLA Ops:
  6.5 403.5 %all-reduce.3.cloned.1.call-start = ((), (), s32[]{:S(2)}) async-start(), calls=%async_computation.2 | async-start | bytes 7340032
Sparse Core Ops, SparseCore 0:
  147.1 262.9 all-reduce.2
where the time goes:
time: 420 us; the launch traced here: 418 us
  waiting for transfers between devices  263 us (63%)
  blocking collectives  110 us (26%)
  local copies, waits for them, and re-layouts  22.2 us (5%)
  between operations  13.4 us (3%)
  matrix products  10.1 us (2%)
    unnamed x2, waiting for transfers between devices  263 us
    all_to_all x1, blocking collectives, shards(): lax.all_to_all(sectioned, 'row', split_axis=3, concat_axis=0, tiled=True)  72.8 us
    all_to_all x1, blocking collectives, shards(): lax.all_to_all(lax.all_to_all(sectioned, 'row', split_axis=3, concat_axis...  36.7 us
    dot_general x1, matrix products, shards(): lax.dot_general(local_amps, flat_ints, (((1,), (1,)), ((), ())), preferre...  10.1 us
  transfers between devices with their start and end apart: 1, of which 1 were waited for; matrix products, arithmetic and copies ran while one was open for 0% of the time, Pallas kernels for 0%

commit v1 on v0

v1 whole, which is shorter than its diff:
```python
import functools

import jax
import jax.numpy as jnp
from jax import lax
from jax.experimental import pallas as pl
from jax.experimental.pallas import tpu as pltpu
from jax.sharding import PartitionSpec as P

MESH = pl.DeviceIdType.MESH
LANES = 128
WIDTH = 2500
TILES = 21
ROWS = 1600
WIDE = 1664
PHASES = 4
SOURCES = 64
CHUNK = 256


def index(z, y, x, k):
    return (z // 2) * 64 + x * 16 + k * 8 + y * 2 + lax.rem(z, 2)


def place(device):
    return {"row": device // 8, "col": lax.rem(device, 8)}


def kernel(
    amps, ints, out, buf, stage, weights, product, pair_in, sums, plane_in, z_out, z_in,
    send20, send21, recv, go, own, load, pair_s, pair_r, plane_s, plane_r, z_s, z_r,
):
    row, col = lax.axis_index("row"), lax.axis_index("col")
    me = row * 8 + col
    z = (row // 8) * 2 + lax.rem(col, 2)
    x = lax.rem(row // 2, 4)
    k = lax.rem(row, 2)
    y = col // 2
    parity = lax.rem(x + y + z, 2)
    phase_me = 2 * k + parity
    xh = x // 2
    slot = ((xh * 4 + y) * 2 + lax.rem(x, 2)) * 4 + z // 2
    mate = index(z, y, x, 1 - k)

    def first_tile(e):
        return (e * WIDTH) // LANES

    def offset(e):
        return lax.rem(e * WIDTH, LANES)

    def remote(src, dst, ssem, rsem, device):
        return pltpu.make_async_remote_copy(src, dst, ssem, rsem, device_id=place(device), device_id_type=MESH)

    barrier = pltpu.get_barrier_semaphore()

    def greet(i, _):
        pl.semaphore_signal(barrier, inc=1, device_id=place(lax.rem(me + i, 256)), device_id_type=MESH)
        return 0

    lax.fori_loop(1, 256, greet, 0)
    shift = offset(me)
    short = shift <= 60
    load_ints = pltpu.make_async_copy(ints, stage, load)
    load_ints.start()

    @pl.when(short)
    def _():
        for p in range(PHASES):
            buf[p, TILES - 1] = jnp.zeros((SOURCES, 2, LANES), jnp.bfloat16)

    def own_copy(n):
        return pltpu.make_async_copy(amps.at[pl.ds(first_tile(me), n)], buf.at[phase_me, pl.ds(0, n), slot], own)

    @pl.when(short)
    def _():
        own_copy(TILES - 1).start()

    @pl.when(jnp.logical_not(short))
    def _():
        own_copy(TILES).start()

    pl.semaphore_wait(barrier, 255)

    def send_all():
        def send(i, _):
            j = lax.rem(i, 8)
            r = i // 8
            half = (j + 1) // 2
            dz = lax.rem(jnp.where(lax.rem(j, 2) == 1, half, 8 - half), 8)
            e = index(lax.rem(z + dz, 8), lax.rem(y + r // 4, 4), lax.rem(x + r, 4), lax.rem(k + r // 16, 2))

            @pl.when(offset(e) <= 60)
            def _():
                remote(amps.at[pl.ds(first_tile(e), TILES - 1)], buf.at[phase_me, pl.ds(0, TILES - 1), slot], send20, recv.at[phase_me], e).start()

            @pl.when(offset(e) > 60)
            def _():
                remote(amps.at[pl.ds(first_tile(e), TILES)], buf.at[phase_me, pl.ds(0, TILES), slot], send21, recv.at[phase_me], e).start()

            return 0

        lax.fori_loop(1, 256, send, 0)

    def sent_all():
        for cond, fewer, more in ((short, 127, 128), (jnp.logical_not(short), 128, 127)):
            @pl.when(cond)
            def _(fewer=fewer, more=more):
                for sem, n in ((send20, fewer * (TILES - 1)), (send21, more * TILES)):
                    part = amps.at[pl.ds(0, n)]
                    remote(part, part, sem, recv.at[0], mate).wait_send()

    @pl.when(phase_me == 0)
    def _():
        send_all()

    load_ints.wait()
    lane = lax.broadcasted_iota(jnp.int32, (32, LANES), 1)
    take = lane >= shift
    tail = lane < WIDTH - 19 * LANES

    for a in range(2):
        def prepare(i, _):
            r = pl.multiple_of(i * 32, 32)
            before = jnp.zeros((32, LANES), jnp.float32)
            for c in range(TILES):
                if c < TILES - 2:
                    v = stage[a, pl.ds(r, 32), c * LANES:(c + 1) * LANES].astype(jnp.float32)
                elif c == TILES - 2:
                    v = stage[a, pl.ds(r, 32), c * LANES:WIDTH].astype(jnp.float32)
                    v = jnp.concatenate([v, jnp.zeros((32, TILES * LANES - LANES - WIDTH), jnp.float32)], axis=1)
                now = pltpu.roll(v, shift, 1) if c < TILES - 1 else jnp.zeros((32, LANES), jnp.float32)
                weights[pl.ds(a * 800 + r, 32), c * LANES:(c + 1) * LANES] = jnp.where(take, now, before).astype(jnp.bfloat16)
                before = now
            return 0

        lax.fori_loop(0, 25, prepare, 0)
    weights[ROWS:, :] = jnp.zeros((WIDE - ROWS, TILES * LANES), jnp.bfloat16)

    def arrived(p):
        for n, cond in ((TILES - 1, short), (TILES, jnp.logical_not(short))):
            def some(count, n=n):
                part = amps.at[pl.ds(0, n * count)]
                remote(part, part, send20, recv.at[p], mate).wait_recv()

            @pl.when(jnp.logical_and(cond, phase_me == p))
            def _(n=n, some=some):
                own_copy(n).wait()
                some(63)

            @pl.when(jnp.logical_and(cond, phase_me != p))
            def _(some=some):
                some(64)

    def multiply(p):
        arrived(p)
        left = jnp.concatenate([buf[p, c].reshape(2 * SOURCES, LANES) for c in range(TILES)], axis=1)
        for n in range(0, WIDE, CHUNK):
            size = min(CHUNK, WIDE - n)
            product[p, :, n:n + size] = lax.dot_general(
                left, weights[n:n + size, :], (((1,), (1,)), ((), ())), preferred_element_type=jnp.float32
            )
            remote(
                product.at[p, pl.ds(pl.multiple_of(64 * (1 - k), 64), 64), pl.ds(n, size)], pair_in.at[p, :, pl.ds(n, size)],
                pair_s, pair_r.at[p], mate,
            ).start()
        remote(pair_in.at[p], pair_in.at[p], pair_s, pair_r.at[p], mate).wait_recv()
        for b in range(8):
            r = pl.multiple_of(64 * k + 8 * b, 8)
            sums[p, b] = product[p, pl.ds(r, 8), :] + pair_in[p, 8 * b:8 * b + 8, :]
            ty, tx = b // 2, 2 * k + b % 2

            @pl.when(jnp.logical_or(ty != y, tx != x))
            def _(b=b, ty=ty, tx=tx):
                remote(sums.at[p, b], plane_in.at[p, y * 4 + x], plane_s, plane_r.at[p], index(z, ty, tx, k)).start()

    def gather(p):
        @pl.when(xh == k)
        def _():
            plane_in[p, y * 4 + x] = sums[p, y * 2 + lax.rem(x, 2)]
            got = plane_in.at[p, pl.ds(0, 15)]
            remote(got, got, plane_s, plane_r.at[p], mate).wait_recv()
            total = plane_in[p, 0]
            for s in range(1, 16):
                total = total + plane_in[p, s]
            kp, q = p // 2, lax.rem(p, 2)
            zl = lax.rem(q + x + y, 2)
            for zh in range(4):
                z_out[4 * p + zh] = total[2 * zh:2 * zh + 2]
                owner = index(2 * zh + zl, y, x, kp)

                @pl.when(owner == me)
                def _(zh=zh):
                    z_in[z] = total[2 * zh:2 * zh + 2]

                @pl.when(owner != me)
                def _(zh=zh, owner=owner):
                    remote(z_out.at[4 * p + zh], z_in.at[z], z_s, z_r, owner).start()

    def step(p, _):
        @pl.when(jnp.logical_and(phase_me == p, p > 0))
        def _():
            pl.semaphore_wait(go, 1)
            send_all()

        @pl.when(jnp.logical_and(p >= 1, p <= PHASES))
        def _():
            multiply(p - 1)

        @pl.when(p >= 2)
        def _():
            gather(p - 2)

        @pl.when(phase_me == p)
        def _():
            sent_all()

            @pl.when(p < PHASES - 1)
            def _():
                follower = index(z, y, x + 1 - 2 * lax.rem(x, 2), (p + 1) // 2)
                pl.semaphore_signal(go, inc=1, device_id=place(follower), device_id_type=MESH)

        return 0

    lax.fori_loop(0, PHASES + 2, step, 0)

    for cond, count in ((xh == k, 7), (xh != k, 8)):
        @pl.when(cond)
        def _(count=count):
            got = z_in.at[pl.ds(0, count)]
            remote(got, got, z_s, z_r, mate).wait_recv()

    total = z_in[0]
    for s in range(1, 8):
        total = total + z_in[s]
    out[:, 0, :] = total[:, 0:800]
    out[:, 1, :] = total[:, 800:1600]

    remote(pair_in, pair_in, pair_s, pair_r.at[0], mate).wait_send()
    for cond, count in ((xh == k, 7), (xh != k, 8)):
        @pl.when(cond)
        def _(count=count):
            part = sums.at[:, pl.ds(0, count)]
            remote(part, part, plane_s, plane_r.at[0], mate).wait_send()

    @pl.when(xh == k)
    def _():
        part = z_out.at[pl.ds(0, 15)]
        remote(part, part, z_s, z_r, mate).wait_send()


def shards(amplitudes, integrals):
    tiles = amplitudes.reshape(2, 5000, LANES).transpose(1, 0, 2)
    dma = pltpu.SemaphoreType.DMA
    return pl.pallas_call(
        kernel,
        out_shape=jax.ShapeDtypeStruct((2, 2, 800), jnp.float32),
        in_specs=[pl.BlockSpec(memory_space=pl.ANY), pl.BlockSpec(memory_space=pl.ANY)],
        out_specs=pl.BlockSpec(memory_space=pltpu.VMEM),
        scratch_shapes=[
            pltpu.VMEM((PHASES, TILES, SOURCES, 2, LANES), jnp.bfloat16),
            pltpu.VMEM((2, 800, WIDTH), jnp.bfloat16),
            pltpu.VMEM((WIDE, TILES * LANES), jnp.bfloat16),
            pltpu.VMEM((PHASES, 128, WIDE), jnp.float32),
            pltpu.VMEM((PHASES, 64, WIDE), jnp.float32),
            pltpu.VMEM((PHASES, 8, 8, WIDE), jnp.float32),
            pltpu.VMEM((PHASES, 16, 8, WIDE), jnp.float32),
            pltpu.VMEM((PHASES * 4, 2, WIDE), jnp.float32),
            pltpu.VMEM((8, 2, WIDE), jnp.float32),
            dma, dma, dma((PHASES,)), pltpu.SemaphoreType.REGULAR, dma, dma,
            dma, dma((PHASES,)), dma, dma((PHASES,)), dma, dma,
        ],
        compiler_params=pltpu.CompilerParams(collective_id=1, has_side_effects=True, vmem_limit_bytes=60 << 20),
        name="ladder",
    )(tiles, integrals)


def solution(mesh):
    return jax.shard_map(
        shards,
        mesh=mesh,
        in_specs=(P(("row", "col"), None), P(None, None, ("row", "col"))),
        out_specs=P(("row", "col"), None, None),
        check_vma=False,
    )
```

time: 420 us -> 134 us (0.32)
  waiting for transfers between devices: 263 us -> 0 us
  Pallas kernels: 0 us -> 130 us
  blocking collectives: 110 us -> 0 us
  local copies, waits for them, and re-layouts: 22.2 us -> 1.31 us
  between operations: 13.4 us -> 0.01 us
  matrix products: 10.1 us -> 0 us
    unnamed x2 -> x0, waiting for transfers between devices: 263 us -> none
    pallas_call x0 -> x1, Pallas kernels: none -> 130 us  [shards(): pl.pallas_call(kernel, out_shape=jax.ShapeDtypeStruct((2, 2, 800), jnp.fl...]
    all_to_all x2 -> x0, blocking collectives: 110 us -> none  [the longest x1 72.8 us: shards(): lax.all_to_all(sectioned, 'row', split_axis=3, concat_axis=0, tiled=True)]
    reshape x3 -> x0, local copies, waits for them, and re-layouts: 11.4 us -> none  [the longest x2 8.23 us: shards(): amplitudes.reshape(1, 1, pair_local, row_count, col_count, slab_width)]
    dot_general x1 -> x0, matrix products: 10.1 us -> none  [shards(): lax.dot_general(local_amps, flat_ints, (((1,), (1,)), ((), ())), preferre...]
    all_to_all x2 -> x0, local copies, waits for them, and re-layouts: 4.51 us -> none  [the longest x1 2.72 us: shards(): lax.all_to_all(lax.all_to_all(sectioned, 'row', split_axis=3, concat_axis...]
    unnamed x2 -> x1, local copies, waits for them, and re-layouts: 5.65 us -> 1.31 us
  transfers between devices with their start and end apart: 1 -> 0, of which waited for: 1 -> 0; matrix products, arithmetic and copies ran while one was open for 0% -> 0% of each run, Pallas kernels for 0% -> 0%
where the time goes in v1:
time: 134 us; the launch traced here: 131 us
  Pallas kernels  130 us (97%)
    pallas_call x1, Pallas kernels, shards(): pl.pallas_call(kernel, out_shape=jax.ShapeDtypeStruct((2, 2, 800), jnp.fl...  130 us

profile of v1, /device:TPU:3, one launch (start us, length us, event | category | flops | bytes accessed | tf_op | source)
XLA Modules:
  0.0 131.5 jit_solution(4553076128553587199)
XLA Ops:
  0.0 130.2 %ladder.1 = f32[2,2,800]{2,1,0:T(2,128)} custom-call(bf16[5000,2,128]{2,1,0:T(2,128)(2,1)} %bitcast.3, bf16[2,800,2500]{2,1,0:T(8,128)(2,1)} %ints.1), custom_call_target="tpu_custom_call" | custom-call | tf_op jit(solution)/shard_map/ladder/pallas_call | solution.py:254
  130.2 1.3 copy.4

commit v2 on v1

v2 whole, which is shorter than its diff:
```python
import functools

import jax
import jax.numpy as jnp
from jax import lax
from jax.experimental import pallas as pl
from jax.experimental.pallas import tpu as pltpu
from jax.sharding import PartitionSpec as P

FLAT = pl.DeviceIdType.LOGICAL
LANES = 128
WIDTH = 2500
TILES = 21
ROWS = 1600
WIDE = 1664
PHASES = 4
SOURCES = 64
CHUNK = 256
CUTS = ((0, 1024), (1024, WIDE))
GO = ("start", "end", "start")


def index(z, y, x, k):
    return (z >> 1) * 64 + x * 16 + k * 8 + y * 2 + (z & 1)


def kernel(
    amps, ints, out, buf, stage, weights, product, pair_in, sums, plane_in, z_out, z_in,
    send_s, recv, go, own, load, pair_s, pair_r, plane_s, plane_r, z_s, z_r,
):
    row, col = lax.axis_index("row"), lax.axis_index("col")
    me = row * 8 + col
    z = (row >> 3) * 2 + (col & 1)
    x = (row >> 1) & 3
    k = row & 1
    y = col >> 1
    parity = (x + y + z) & 1
    phase_me = 2 * k + parity
    xh = x >> 1
    slot = ((xh * 4 + y) * 2 + (x & 1)) * 4 + (z >> 1)
    mate = index(z, y, x, 1 - k)

    def first_tile(e):
        return (e * WIDTH) >> 7

    def offset(e):
        return (e * WIDTH) & (LANES - 1)

    def remote(src, dst, ssem, rsem, device):
        return pltpu.make_async_remote_copy(src, dst, ssem, rsem, device_id=device, device_id_type=FLAT)

    barrier = pltpu.get_barrier_semaphore()

    def greet(i, _):
        gz, gy = i >> 3, (i >> 1) & 3
        e = index(gz, gy, (i & 1) * 2 + ((gy + gz) & 1), 0)

        @pl.when(e != me)
        def _():
            pl.semaphore_signal(barrier, inc=1, device_id=e, device_id_type=FLAT)

        return 0

    lax.fori_loop(0, SOURCES, greet, 0)
    shift = offset(me)
    short = shift <= 60
    load_ints = pltpu.make_async_copy(ints, stage, load)
    load_ints.start()

    @pl.when(short)
    def _():
        for p in range(PHASES):
            buf[p, TILES - 1] = jnp.zeros((SOURCES, 2, LANES), jnp.bfloat16)

    def own_copy(n):
        return pltpu.make_async_copy(amps.at[pl.ds(first_tile(me), n)], buf.at[phase_me, pl.ds(0, n), slot], own)

    @pl.when(short)
    def _():
        own_copy(TILES - 1).start()

    @pl.when(jnp.logical_not(short))
    def _():
        own_copy(TILES).start()

    @pl.when(phase_me == 0)
    def _():
        pl.semaphore_wait(barrier, 255)

    def send(e, half):
        def some(n, kind):
            remote(
                amps.at[pl.ds(first_tile(e), n)], buf.at[phase_me, pl.ds(0, n), slot], send_s.at[half, kind], recv.at[phase_me], e
            ).start()

        lax.cond(offset(e) <= 60, lambda: some(TILES - 1, 0), lambda: some(TILES, 1))

    def send_all():
        layers = [index((z + dz) & 7, 0, 0, 0) for dz in (1, 7, 2, 6, 3, 5, 4, 0)]
        for layer in layers[:7]:
            send(layer + index(0, y, x, k), 0)
        for half in range(2):
            def plane(r, _, half=half):
                base = index(0, (y + (r >> 2)) & 3, (x + r) & 3, (k + half) & 1)
                for layer in layers:
                    send(layer + base, half)
                return 0

            lax.fori_loop(1 - half, 16, plane, 0)

    def sent(half):
        for cond, fewer, more in ((short, 63, 64), (jnp.logical_not(short), 64, 63)):
            @pl.when(cond)
            def _(fewer=fewer, more=more):
                for kind, n in ((0, (64 if half else fewer) * (TILES - 1)), (1, (64 if half else more) * TILES)):
                    part = amps.at[pl.ds(0, n)]
                    remote(part, part, send_s.at[half, kind], recv.at[0], mate).wait_send()

    def pass_on(p):
        follower = index(z, y, x + 1 - 2 * (x & 1), (p + 1) >> 1)
        pl.semaphore_signal(go, inc=1, device_id=follower, device_id_type=FLAT)

    @pl.when(phase_me == 0)
    def _():
        if GO[0] == "start":
            pass_on(0)
        send_all()

    load_ints.wait()

    def prepare(r, count):
        lane = lax.broadcasted_iota(jnp.int32, (count, LANES), 1)
        take = lane >= shift
        before = jnp.zeros((count, LANES), jnp.float32)
        for c in range(TILES):
            if c < TILES - 2:
                v = stage[pl.ds(r, count), c * LANES:(c + 1) * LANES].astype(jnp.float32)
            elif c == TILES - 2:
                v = stage[pl.ds(r, count), c * LANES:WIDTH].astype(jnp.float32)
                v = jnp.concatenate([v, jnp.zeros((count, TILES * LANES - LANES - WIDTH), jnp.float32)], axis=1)
            now = pltpu.roll(v, shift, 1) if c < TILES - 1 else jnp.zeros((count, LANES), jnp.float32)
            block = jnp.where(take, now, before)
            if count < LANES:
                block = jnp.concatenate([block, jnp.zeros((LANES - count, LANES), jnp.float32)], axis=0)
            weights[c * LANES:(c + 1) * LANES, pl.ds(r, LANES)] = block.T.astype(jnp.bfloat16)
            before = now

    def prepare_block(i, _):
        prepare(pl.multiple_of(i * LANES, LANES), LANES)
        return 0

    lax.fori_loop(0, ROWS // LANES, prepare_block, 0)
    prepare(ROWS // LANES * LANES, ROWS % LANES)

    def arrived(p):
        for n, cond in ((TILES - 1, short), (TILES, jnp.logical_not(short))):
            def some(count, n=n):
                part = amps.at[pl.ds(0, n * count)]
                remote(part, part, send_s.at[0, 0], recv.at[p], mate).wait_recv()

            @pl.when(jnp.logical_and(cond, phase_me == p))
            def _(n=n, some=some):
                own_copy(n).wait()
                some(63)

            @pl.when(jnp.logical_and(cond, phase_me != p))
            def _(some=some):
                some(64)

    def multiply(p):
        arrived(p)
        left = jnp.concatenate([buf[p, c].reshape(2 * SOURCES, LANES) for c in range(TILES)], axis=1)
        theirs = pl.multiple_of(64 * (1 - k), 64)
        for cut, (lo, hi) in enumerate(CUTS):
            for n in range(lo, hi, CHUNK):
                size = min(CHUNK, hi - n)
                product[p, :, n:n + size] = jnp.dot(left, weights[:, n:n + size], preferred_element_type=jnp.float32)
            remote(
                product.at[p, pl.ds(theirs, 64), pl.ds(lo, hi - lo)], pair_in.at[p, :, pl.ds(lo, hi - lo)],
                pair_s, pair_r.at[p, cut], mate,
            ).start()
        for cut, (lo, hi) in enumerate(CUTS):
            got = pair_in.at[p, :, pl.ds(lo, hi - lo)]
            remote(got, got, pair_s, pair_r.at[p, cut], mate).wait_recv()
            for b in range(8):
                r = pl.multiple_of(64 * k + 8 * b, 8)
                sums[p, b, :, lo:hi] = product[p, pl.ds(r, 8), lo:hi] + pair_in[p, 8 * b:8 * b + 8, lo:hi]
                ty, tx = b // 2, 2 * k + b % 2

                @pl.when(jnp.logical_or(ty != y, tx != x))
                def _(b=b, ty=ty, tx=tx):
                    remote(
                        sums.at[p, b, :, pl.ds(lo, hi - lo)], plane_in.at[p, y * 4 + x, :, pl.ds(lo, hi - lo)],
                        plane_s, plane_r.at[p, cut], index(z, ty, tx, k),
                    ).start()

    def gather(p):
        @pl.when(xh == k)
        def _():
            plane_in[p, y * 4 + x] = sums[p, y * 2 + (x & 1)]
            for cut, (lo, hi) in enumerate(CUTS):
                got = plane_in.at[p, pl.ds(0, 15), :, pl.ds(lo, hi - lo)]
                remote(got, got, plane_s, plane_r.at[p, cut], mate).wait_recv()
            total = plane_in[p, 0]
            for s in range(1, 16):
                total = total + plane_in[p, s]
            kp, q = p >> 1, p & 1
            zl = (q + x + y) & 1
            for zh in range(4):
                z_out[4 * p + zh] = total[2 * zh:2 * zh + 2]
                owner = index(2 * zh + zl, y, x, kp)

                @pl.when(owner == me)
                def _(zh=zh):
                    z_in[z] = total[2 * zh:2 * zh + 2]

                @pl.when(owner != me)
                def _(zh=zh, owner=owner):
                    remote(z_out.at[4 * p + zh], z_in.at[z], z_s, z_r, owner).start()

    def step(p, _):
        @pl.when(jnp.logical_and(phase_me == p, p > 0))
        def _():
            pl.semaphore_wait(go, 1)
            for q in range(1, PHASES - 1):
                if GO[q] == "start":
                    @pl.when(p == q)
                    def _(q=q):
                        pass_on(q)
            send_all()

        @pl.when(jnp.logical_and(p >= 1, p <= PHASES))
        def _():
            multiply(p - 1)

        @pl.when(phase_me == p)
        def _():
            sent(0)
            for q in range(PHASES - 1):
                if GO[q] == "half":
                    @pl.when(p == q)
                    def _(q=q):
                        pass_on(q)
            sent(1)
            for q in range(PHASES - 1):
                if GO[q] == "end":
                    @pl.when(p == q)
                    def _(q=q):
                        pass_on(q)

        @pl.when(p >= 2)
        def _():
            gather(p - 2)

        return 0

    lax.fori_loop(0, PHASES + 2, step, 0)

    for cond, count in ((xh == k, 7), (xh != k, 8)):
        @pl.when(cond)
        def _(count=count):
            got = z_in.at[pl.ds(0, count)]
            remote(got, got, z_s, z_r, mate).wait_recv()

    total = z_in[0]
    for s in range(1, 8):
        total = total + z_in[s]
    out[:, 0, :] = total[:, 0:800]
    out[:, 1, :] = total[:, 800:1600]

    remote(pair_in, pair_in, pair_s, pair_r.at[0, 0], mate).wait_send()
    for cond, count in ((xh == k, 7), (xh != k, 8)):
        @pl.when(cond)
        def _(count=count):
            part = sums.at[:, pl.ds(0, count)]
            remote(part, part, plane_s, plane_r.at[0, 0], mate).wait_send()

    @pl.when(xh == k)
    def _():
        part = z_out.at[pl.ds(0, 15)]
        remote(part, part, z_s, z_r, mate).wait_send()


def shards(amplitudes, integrals):
    tiles = amplitudes.reshape(2, 5000, LANES).transpose(1, 0, 2)
    dma = pltpu.SemaphoreType.DMA
    return pl.pallas_call(
        kernel,
        out_shape=jax.ShapeDtypeStruct((2, 2, 800), jnp.float32),
        in_specs=[pl.BlockSpec(memory_space=pl.ANY), pl.BlockSpec(memory_space=pl.ANY)],
        out_specs=pl.BlockSpec(memory_space=pltpu.VMEM),
        scratch_shapes=[
            pltpu.VMEM((PHASES, TILES, SOURCES, 2, LANES), jnp.bfloat16),
            pltpu.VMEM((ROWS, WIDTH), jnp.bfloat16),
            pltpu.VMEM((TILES * LANES, WIDE), jnp.bfloat16),
            pltpu.VMEM((PHASES, 128, WIDE), jnp.float32),
            pltpu.VMEM((PHASES, 64, WIDE), jnp.float32),
            pltpu.VMEM((PHASES, 8, 8, WIDE), jnp.float32),
            pltpu.VMEM((PHASES, 16, 8, WIDE), jnp.float32),
            pltpu.VMEM((PHASES * 4, 2, WIDE), jnp.float32),
            pltpu.VMEM((8, 2, WIDE), jnp.float32),
            dma((2, 2)), dma((PHASES,)), pltpu.SemaphoreType.REGULAR, dma, dma,
            dma, dma((PHASES, 2)), dma, dma((PHASES, 2)), dma, dma,
        ],
        compiler_params=pltpu.CompilerParams(collective_id=1, has_side_effects=True, vmem_limit_bytes=60 << 20),
        name="ladder",
    )(tiles, integrals.reshape(ROWS, WIDTH))


def solution(mesh):
    return jax.shard_map(
        shards,
        mesh=mesh,
        in_specs=(P(("row", "col"), None), P(None, None, ("row", "col"))),
        out_specs=P(("row", "col"), None, None),
        check_vma=False,
    )
```

time: 134 us -> 103 us (0.77); the launches traced: 131 us -> 103 us
  Pallas kernels: 130 us -> 102 us
    pallas_call x1, Pallas kernels: 130 us -> 102 us  [shards(): pl.pallas_call(kernel, out_shape=jax.ShapeDtypeStruct((2, 2, 800), jnp.fl...]
where the time goes in v2:
time: 103 us
  Pallas kernels  102 us (99%)
  local copies, waits for them, and re-layouts  1.31 us (1%)
    pallas_call x1, Pallas kernels, shards(): pl.pallas_call(kernel, out_shape=jax.ShapeDtypeStruct((2, 2, 800), jnp.fl...  102 us

profile of v2, /device:TPU:3, one launch (start us, length us, event | category | flops | bytes accessed | tf_op | source)
XLA Modules:
  0.0 103.0 jit_solution(9434716316934468167)
XLA Ops:
  0.0 101.7 %ladder.1 = f32[2,2,800]{2,1,0:T(2,128)} custom-call(bf16[5000,2,128]{2,1,0:T(2,128)(2,1)} %bitcast.5, bf16[1600,2500]{1,0:T(8,128)(2,1)} %bitcast.4), custom_call_target="tpu_custom_call" | custom-call | tf_op jit(solution)/shard_map/ladder/pallas_call | solution.py:287
  101.7 1.3 %copy.4 = f32[2,2,800]{2,1,0:T(2,128)} copy(f32[2,2,800]{2,1,0:T(2,128)} %ladder.1) | data formatting | bytes 25600

commit v3 on v2

--- a/solution.py
+++ b/solution.py
@@ -16,8 +16,9 @@
 PHASES = 4
 SOURCES = 64
 CHUNK = 256
-CUTS = ((0, 1024), (1024, WIDE))
-GO = ("start", "end", "start")
+CUTS = ((0, 768), (768, WIDE))
+FIRST = 28
+WAITS = (0, 0)
 
 
 def index(z, y, x, k):
@@ -25,8 +26,8 @@
 
 
 def kernel(
-    amps, ints, out, buf, stage, weights, product, pair_in, sums, plane_in, z_out, z_in,
-    send_s, recv, go, own, load, pair_s, pair_r, plane_s, plane_r, z_s, z_r,
+    amps, ints, out, buf, stage, weights, product, pair_in, x_out, x_in, xy_out, xy_in, y_out, y_in, yx_out, yx_in, z_out, z_in,
+    send_s, recv, go, own, load, pair_s, pair_r, x_s, x_r, xy_s, xy_r, y_s, y_r, yx_s, yx_r, z_s, z_r,
 ):
     row, col = lax.axis_index("row"), lax.axis_index("col")
     me = row * 8 + col
@@ -96,34 +97,47 @@
         lax.cond(offset(e) <= 60, lambda: some(TILES - 1, 0), lambda: some(TILES, 1))
 
     def send_all():
-        layers = [index((z + dz) & 7, 0, 0, 0) for dz in (1, 7, 2, 6, 3, 5, 4, 0)]
-        for layer in layers[:7]:
-            send(layer + index(0, y, x, k), 0)
-        for half in range(2):
-            def plane(r, _, half=half):
-                base = index(0, (y + (r >> 2)) & 3, (x + r) & 3, (k + half) & 1)
-                for layer in layers:
-                    send(layer + base, half)
+        near = [[index((z + dz) & 7, 0, 0, 0) for dz in pair] for pair in ((1, 7), (2, 6), (3, 5), (4, 0))]
+        turns = (5, 10, 15, 0)
+
+        def group(i, part, first=False):
+            for pair, turn in zip(near, turns):
+                r = i + turn
+                base = index(0, (y + r + ((r & 15) >> 2)) & 3, (x + r) & 3, (k + (i >> 4)) & 1)
+                for layer in pair[:1] if first and turn == 0 else pair:
+                    send(layer + base, part)
+
+        group(0, 0, True)
+        for part, (lo, hi) in enumerate(((1, FIRST), (FIRST, 32))):
+            def turn(i, _, part=part):
+                group(i, part)
                 return 0
 
-            lax.fori_loop(1 - half, 16, plane, 0)
-
-    def sent(half):
-        for cond, fewer, more in ((short, 63, 64), (jnp.logical_not(short), 64, 63)):
+            lax.fori_loop(lo, hi, turn, 0)
+
+    def sent(part):
+        count = (4 * FIRST, 128 - 4 * FIRST)[part]
+        for cond, fewer in ((short, 0), (jnp.logical_not(short), 1)):
             @pl.when(cond)
-            def _(fewer=fewer, more=more):
-                for kind, n in ((0, (64 if half else fewer) * (TILES - 1)), (1, (64 if half else more) * TILES)):
-                    part = amps.at[pl.ds(0, n)]
-                    remote(part, part, send_s.at[half, kind], recv.at[0], mate).wait_send()
-
-    def pass_on(p):
-        follower = index(z, y, x + 1 - 2 * (x & 1), (p + 1) >> 1)
-        pl.semaphore_signal(go, inc=1, device_id=follower, device_id_type=FLAT)
+            def _(fewer=fewer):
+                for kind, n in ((0, TILES - 1), (1, TILES)):
+                    less = 1 if part == 0 and kind == fewer else 0
+                    moved = amps.at[pl.ds(0, n * (count - less))]
+                    remote(moved, moved, send_s.at[part, kind], recv.at[0], mate).wait_send()
+
+    def signal(device):
+        pl.semaphore_signal(go, inc=1, device_id=device, device_id_type=FLAT)
 
     @pl.when(phase_me == 0)
     def _():
-        if GO[0] == "start":
-            pass_on(0)
+        signal(index(z, y, x + 1 - 2 * (x & 1), 0))
+
+    @pl.when(phase_me == 1)
+    def _():
+        pl.semaphore_wait(go, 1)
+
+    @pl.when(k == 0)
+    def _():
         send_all()
 
     load_ints.wait()
@@ -179,31 +193,73 @@
                 product.at[p, pl.ds(theirs, 64), pl.ds(lo, hi - lo)], pair_in.at[p, :, pl.ds(lo, hi - lo)],
                 pair_s, pair_r.at[p, cut], mate,
             ).start()
+
+    def combine(p):
         for cut, (lo, hi) in enumerate(CUTS):
             got = pair_in.at[p, :, pl.ds(lo, hi - lo)]
             remote(got, got, pair_s, pair_r.at[p, cut], mate).wait_recv()
-            for b in range(8):
-                r = pl.multiple_of(64 * k + 8 * b, 8)
-                sums[p, b, :, lo:hi] = product[p, pl.ds(r, 8), lo:hi] + pair_in[p, 8 * b:8 * b + 8, lo:hi]
-                ty, tx = b // 2, 2 * k + b % 2
-
-                @pl.when(jnp.logical_or(ty != y, tx != x))
-                def _(b=b, ty=ty, tx=tx):
-                    remote(
-                        sums.at[p, b, :, pl.ds(lo, hi - lo)], plane_in.at[p, y * 4 + x, :, pl.ds(lo, hi - lo)],
-                        plane_s, plane_r.at[p, cut], index(z, ty, tx, k),
-                    ).start()
+            for ty in range(4):
+                for xl in range(2):
+                    r = 16 * ty + 8 * xl
+                    total = product[p, pl.ds(pl.multiple_of(64 * k + r, 8), 8), lo:hi] + pair_in[p, r:r + 8, lo:hi]
+                    if cut == 0:
+                        x_out[p, xl, ty] = total
+                    else:
+                        y_out[p, ty, xl] = total
+            if cut == 0:
+                for xl in range(2):
+                    @pl.when(2 * k + xl != x)
+                    def _(xl=xl):
+                        remote(x_out.at[p, xl], x_in.at[p, x], x_s, x_r.at[p], index(z, y, 2 * k + xl, k)).start()
+            else:
+                for ty in range(4):
+                    @pl.when(ty != y)
+                    def _(ty=ty):
+                        remote(y_out.at[p, ty], y_in.at[p, y], y_s, y_r.at[p], index(z, ty, x, k)).start()
+
+    def received(n, sem):
+        part = amps.at[pl.ds(0, n)]
+        remote(part, part, pair_s, sem, mate).wait_recv()
+
+    def departed(n, sem):
+        part = amps.at[pl.ds(0, n)]
+        remote(part, part, sem, pair_r.at[0, 0], mate).wait_send()
+
+    X, Y = CUTS[0][1], WIDE - CUTS[0][1]
+
+    def middle(p):
+        @pl.when(xh == k)
+        def _():
+            x_in[p, x] = x_out[p, x & 1]
+            received(3 * X // 4, x_r.at[p])
+            for ty in range(4):
+                total = (x_in[p, 0, ty] + x_in[p, 1, ty]) + (x_in[p, 2, ty] + x_in[p, 3, ty])
+                xy_out[p, ty] = total
+
+                @pl.when(ty != y)
+                def _(ty=ty):
+                    remote(xy_out.at[p, ty], xy_in.at[p, y], xy_s, xy_r.at[p], index(z, ty, x, k)).start()
+
+        y_in[p, y] = y_out[p, y]
+        received(3 * Y // 8, y_r.at[p])
+        for xl in range(2):
+            total = (y_in[p, 0, xl] + y_in[p, 1, xl]) + (y_in[p, 2, xl] + y_in[p, 3, xl])
+            yx_out[p, xl] = total
+
+            @pl.when(2 * k + xl != x)
+            def _(xl=xl):
+                remote(yx_out.at[p, xl], yx_in.at[p, x], yx_s, yx_r.at[p], index(z, y, 2 * k + xl, k)).start()
 
     def gather(p):
         @pl.when(xh == k)
         def _():
-            plane_in[p, y * 4 + x] = sums[p, y * 2 + (x & 1)]
-            for cut, (lo, hi) in enumerate(CUTS):
-                got = plane_in.at[p, pl.ds(0, 15), :, pl.ds(lo, hi - lo)]
-                remote(got, got, plane_s, plane_r.at[p, cut], mate).wait_recv()
-            total = plane_in[p, 0]
-            for s in range(1, 16):
-                total = total + plane_in[p, s]
+            xy_in[p, y] = xy_out[p, y]
+            yx_in[p, x] = yx_out[p, x & 1]
+            received(3 * X // 16, xy_r.at[p])
+            received(3 * Y // 16, yx_r.at[p])
+            first = (xy_in[p, 0] + xy_in[p, 1]) + (xy_in[p, 2] + xy_in[p, 3])
+            second = (yx_in[p, 0] + yx_in[p, 1]) + (yx_in[p, 2] + yx_in[p, 3])
+            total = jnp.concatenate([first, second], axis=1)
             kp, q = p >> 1, p & 1
             zl = (q + x + y) & 1
             for zh in range(4):
@@ -218,43 +274,51 @@
                 def _(zh=zh, owner=owner):
                     remote(z_out.at[4 * p + zh], z_in.at[z], z_s, z_r, owner).start()
 
-    def step(p, _):
-        @pl.when(jnp.logical_and(phase_me == p, p > 0))
-        def _():
-            pl.semaphore_wait(go, 1)
-            for q in range(1, PHASES - 1):
-                if GO[q] == "start":
-                    @pl.when(p == q)
-                    def _(q=q):
-                        pass_on(q)
-            send_all()
-
-        @pl.when(jnp.logical_and(p >= 1, p <= PHASES))
-        def _():
-            multiply(p - 1)
-
-        @pl.when(phase_me == p)
-        def _():
-            sent(0)
-            for q in range(PHASES - 1):
-                if GO[q] == "half":
-                    @pl.when(p == q)
-                    def _(q=q):
-                        pass_on(q)
-            sent(1)
-            for q in range(PHASES - 1):
-                if GO[q] == "end":
-                    @pl.when(p == q)
-                    def _(q=q):
-                        pass_on(q)
-
-        @pl.when(p >= 2)
-        def _():
-            gather(p - 2)
-
-        return 0
-
-    lax.fori_loop(0, PHASES + 2, step, 0)
+    @pl.when(k == 0)
+    def _():
+        sent(0)
+        for q in range(2):
+            @pl.when(parity == q)
+            def _(q=q):
+                if WAITS[q] == 0:
+                    signal(mate)
+                    sent(1)
+                else:
+                    sent(1)
+                    signal(mate)
+
+    @pl.when(k == 1)
+    def _():
+        pl.semaphore_wait(go, 1)
+        send_all()
+
+    def each(f, lo):
+        def one(p, _):
+            f(p)
+            return 0
+
+        lax.fori_loop(lo, lo + 2, one, 0)
+
+    each(multiply, 0)
+    each(combine, 0)
+    each(middle, 0)
+
+    def both(p):
+        multiply(p)
+        combine(p)
+
+    @pl.when(k == 0)
+    def _():
+        each(both, 2)
+
+    @pl.when(k == 1)
+    def _():
+        each(multiply, 2)
+        each(combine, 2)
+
+    each(gather, 0)
+    each(middle, 2)
+    each(gather, 2)
 
     for cond, count in ((xh == k, 7), (xh != k, 8)):
         @pl.when(cond)
@@ -268,12 +332,22 @@
     out[:, 0, :] = total[:, 0:800]
     out[:, 1, :] = total[:, 800:1600]
 
+    @pl.when(k == 1)
+    def _():
+        sent(0)
+        sent(1)
+
     remote(pair_in, pair_in, pair_s, pair_r.at[0, 0], mate).wait_send()
-    for cond, count in ((xh == k, 7), (xh != k, 8)):
+    departed(4 * 3 * Y // 8, y_s)
+    for cond, count in ((xh == k, 1), (xh != k, 2)):
         @pl.when(cond)
         def _(count=count):
-            part = sums.at[:, pl.ds(0, count)]
-            remote(part, part, plane_s, plane_r.at[0, 0], mate).wait_send()
+            departed(4 * count * X // 4, x_s)
+            departed(4 * count * Y // 16, yx_s)
+
+    @pl.when(xh == k)
+    def _():
+        departed(4 * 3 * X // 16, xy_s)
 
     @pl.when(xh == k)
     def _():
@@ -295,12 +369,18 @@
             pltpu.VMEM((TILES * LANES, WIDE), jnp.bfloat16),
             pltpu.VMEM((PHASES, 128, WIDE), jnp.float32),
             pltpu.VMEM((PHASES, 64, WIDE), jnp.float32),
-            pltpu.VMEM((PHASES, 8, 8, WIDE), jnp.float32),
-            pltpu.VMEM((PHASES, 16, 8, WIDE), jnp.float32),
+            pltpu.VMEM((PHASES, 2, 4, 8, CUTS[0][1]), jnp.float32),
+            pltpu.VMEM((PHASES, 4, 4, 8, CUTS[0][1]), jnp.float32),
+            pltpu.VMEM((PHASES, 4, 8, CUTS[0][1]), jnp.float32),
+            pltpu.VMEM((PHASES, 4, 8, CUTS[0][1]), jnp.float32),
+            pltpu.VMEM((PHASES, 4, 2, 8, WIDE - CUTS[0][1]), jnp.float32),
+            pltpu.VMEM((PHASES, 4, 2, 8, WIDE - CUTS[0][1]), jnp.float32),
+            pltpu.VMEM((PHASES, 2, 8, WIDE - CUTS[0][1]), jnp.float32),
+            pltpu.VMEM((PHASES, 4, 8, WIDE - CUTS[0][1]), jnp.float32),
             pltpu.VMEM((PHASES * 4, 2, WIDE), jnp.float32),
             pltpu.VMEM((8, 2, WIDE), jnp.float32),
             dma((2, 2)), dma((PHASES,)), pltpu.SemaphoreType.REGULAR, dma, dma,
-            dma, dma((PHASES, 2)), dma, dma((PHASES, 2)), dma, dma,
+            dma, dma((PHASES, 2)), dma, dma((PHASES,)), dma, dma((PHASES,)), dma, dma((PHASES,)), dma, dma((PHASES,)), dma, dma,
         ],
         compiler_params=pltpu.CompilerParams(collective_id=1, has_side_effects=True, vmem_limit_bytes=60 << 20),
         name="ladder",

time: 103 us -> 95.3 us (0.925)
  Pallas kernels: 102 us -> 93.8 us
    pallas_call x1, Pallas kernels: 102 us -> 93.8 us  [shards(): pl.pallas_call(kernel, out_shape=jax.ShapeDtypeStruct((2, 2, 800), jnp.fl...]
where the time goes in v3:
time: 95.3 us; the launch traced here: 95.1 us
  Pallas kernels  93.8 us (98%)
  local copies, waits for them, and re-layouts  1.31 us (1%)
    pallas_call x1, Pallas kernels, shards(): pl.pallas_call(kernel, out_shape=jax.ShapeDtypeStruct((2, 2, 800), jnp.fl...  93.8 us

profile of v3, /device:TPU:3, one launch (start us, length us, event | category | flops | bytes accessed | tf_op | source)
XLA Modules:
  0.0 95.1 jit_solution(9679511618405367726)
XLA Ops:
  0.0 93.8 %ladder.1 = f32[2,2,800]{2,1,0:T(2,128)} custom-call(bf16[5000,2,128]{2,1,0:T(2,128)(2,1)} %bitcast.5, bf16[1600,2500]{1,0:T(8,128)(2,1)} %bitcast.4), custom_call_target="tpu_custom_call" | custom-call | tf_op jit(solution)/shard_map/ladder/pallas_call | solution.py:361
  93.8 1.3 %copy.4 = f32[2,2,800]{2,1,0:T(2,128)} copy(f32[2,2,800]{2,1,0:T(2,128)} %ladder.1) | data formatting | bytes 25600

commit v4 on v3

--- a/solution.py
+++ b/solution.py
@@ -10,15 +10,13 @@
 FLAT = pl.DeviceIdType.LOGICAL
 LANES = 128
 WIDTH = 2500
-TILES = 21
+TILES = 20
 ROWS = 1600
 WIDE = 1664
 PHASES = 4
 SOURCES = 64
 CHUNK = 256
 CUTS = ((0, 768), (768, WIDE))
-FIRST = 28
-WAITS = (0, 0)
 
 
 def index(z, y, x, k):
@@ -26,8 +24,8 @@
 
 
 def kernel(
-    amps, ints, out, buf, stage, weights, product, pair_in, x_out, x_in, xy_out, xy_in, y_out, y_in, yx_out, yx_in, z_out, z_in,
-    send_s, recv, go, own, load, pair_s, pair_r, x_s, x_r, xy_s, xy_r, y_s, y_r, yx_s, yx_r, z_s, z_r,
+    amps, ints, out, buf, merged, stage, weights, product, pair_in, x_out, x_in, xy_out, xy_in, y_out, y_in, yx_out, yx_in, z_out, z_in,
+    send_s, recv, go, own, load, load_tiles, pair_s, pair_r, x_s, x_r, xy_s, xy_r, y_s, y_r, yx_s, yx_r, z_s, z_r,
 ):
     row, col = lax.axis_index("row"), lax.axis_index("col")
     me = row * 8 + col
@@ -64,66 +62,88 @@
 
     lax.fori_loop(0, SOURCES, greet, 0)
     shift = offset(me)
-    short = shift <= 60
     load_ints = pltpu.make_async_copy(ints, stage, load)
+    odd = (x + z) & 1
+
+    def fetch(j, _):
+        e = 2 * j + 1 - ((j >> 3) & 1)
+        pltpu.make_async_copy(amps.at[pl.ds(first_tile(e), TILES + 1)], merged.at[j >> 4, j & 15], load_tiles).start()
+        return 0
+
+    def merge():
+        part = amps.at[pl.ds(0, 128 * (TILES + 1))]
+        pltpu.make_async_copy(part, part, load_tiles).wait()
+        lane = lax.broadcasted_iota(jnp.int32, (8, 2, LANES), 2)
+        for j in range(16):
+            first = lane >= ((2 * j + 1 - (j >> 3)) * WIDTH) % LANES
+            head, last = merged[:, j, 0].astype(jnp.float32), merged[:, j, TILES].astype(jnp.float32)
+            merged[:, j, 0] = jnp.where(first, head, last).astype(jnp.bfloat16)
+
+    def straight(e):
+        return amps.at[pl.ds(first_tile(e), TILES)]
+
+    def folded(e):
+        return merged.at[e >> 5, (e >> 1) & 15, pl.ds(0, TILES)]
+
+    def own_copy(src):
+        return pltpu.make_async_copy(src, buf.at[phase_me, :, slot], own)
+
+    def send_some(lo, hi, core, fold, part):
+        near = [[index((z + dz) & 7, 0, 0, 0) for dz in pair] for pair in ((1, 7), (2, 6), (3, 5), (4, 0))]
+
+        def group(m, last):
+            i = 2 * m + (odd ^ fold)
+            for pair, turn in zip(near, (5, 10, 15, 0)):
+                r = i + turn
+                base = index(0, (y + r + ((r & 15) >> 2)) & 3, (x + r) & 3, (k + core) & 1)
+                for number, layer in enumerate(pair):
+                    e = layer + base
+
+                    def go_to(e=e):
+                        src = folded(e) if fold else straight(e)
+                        remote(src, buf.at[phase_me, :, slot], send_s.at[part], recv.at[phase_me], e).start()
+
+                    if last and turn == 0 and number == 1:
+                        pl.when(e != me)(go_to)
+                    else:
+                        go_to()
+
+        if lo == 0:
+            group(0, core == 0)
+
+        def one(m, _):
+            group(m, False)
+            return 0
+
+        lax.fori_loop(max(lo, 1), hi, one, 0)
+
+    def send_all():
+        send_some(0, 8, 0, 0, 0)
+        merge()
+
+        @pl.when(odd == 1)
+        def _():
+            own_copy(folded(me)).start()
+
+        @pl.when(odd == 0)
+        def _():
+            own_copy(straight(me)).start()
+
+        send_some(0, 8, 0, 1, 0)
+        send_some(0, 8, 1, 0, 0)
+        send_some(0, 4, 1, 1, 0)
+        send_some(4, 8, 1, 1, 1)
+
+    def sent(part):
+        gone = amps.at[pl.ds(0, (223, 32)[part] * TILES)]
+        remote(gone, gone, send_s.at[part], recv.at[0], mate).wait_send()
+
     load_ints.start()
-
-    @pl.when(short)
-    def _():
-        for p in range(PHASES):
-            buf[p, TILES - 1] = jnp.zeros((SOURCES, 2, LANES), jnp.bfloat16)
-
-    def own_copy(n):
-        return pltpu.make_async_copy(amps.at[pl.ds(first_tile(me), n)], buf.at[phase_me, pl.ds(0, n), slot], own)
-
-    @pl.when(short)
-    def _():
-        own_copy(TILES - 1).start()
-
-    @pl.when(jnp.logical_not(short))
-    def _():
-        own_copy(TILES).start()
+    lax.fori_loop(0, 128, fetch, 0)
 
     @pl.when(phase_me == 0)
     def _():
         pl.semaphore_wait(barrier, 255)
-
-    def send(e, half):
-        def some(n, kind):
-            remote(
-                amps.at[pl.ds(first_tile(e), n)], buf.at[phase_me, pl.ds(0, n), slot], send_s.at[half, kind], recv.at[phase_me], e
-            ).start()
-
-        lax.cond(offset(e) <= 60, lambda: some(TILES - 1, 0), lambda: some(TILES, 1))
-
-    def send_all():
-        near = [[index((z + dz) & 7, 0, 0, 0) for dz in pair] for pair in ((1, 7), (2, 6), (3, 5), (4, 0))]
-        turns = (5, 10, 15, 0)
-
-        def group(i, part, first=False):
-            for pair, turn in zip(near, turns):
-                r = i + turn
-                base = index(0, (y + r + ((r & 15) >> 2)) & 3, (x + r) & 3, (k + (i >> 4)) & 1)
-                for layer in pair[:1] if first and turn == 0 else pair:
-                    send(layer + base, part)
-
-        group(0, 0, True)
-        for part, (lo, hi) in enumerate(((1, FIRST), (FIRST, 32))):
-            def turn(i, _, part=part):
-                group(i, part)
-                return 0
-
-            lax.fori_loop(lo, hi, turn, 0)
-
-    def sent(part):
-        count = (4 * FIRST, 128 - 4 * FIRST)[part]
-        for cond, fewer in ((short, 0), (jnp.logical_not(short), 1)):
-            @pl.when(cond)
-            def _(fewer=fewer):
-                for kind, n in ((0, TILES - 1), (1, TILES)):
-                    less = 1 if part == 0 and kind == fewer else 0
-                    moved = amps.at[pl.ds(0, n * (count - less))]
-                    remote(moved, moved, send_s.at[part, kind], recv.at[0], mate).wait_send()
 
     def signal(device):
         pl.semaphore_signal(go, inc=1, device_id=device, device_id_type=FLAT)
@@ -143,16 +163,17 @@
     load_ints.wait()
 
     def prepare(r, count):
-        lane = lax.broadcasted_iota(jnp.int32, (count, LANES), 1)
-        take = lane >= shift
-        before = jnp.zeros((count, LANES), jnp.float32)
+        take = lax.broadcasted_iota(jnp.int32, (count, LANES), 1) >= shift
+
+        def turned(c):
+            v = stage[pl.ds(r, count), c * LANES:min((c + 1) * LANES, WIDTH)].astype(jnp.float32)
+            if c == TILES - 1:
+                v = jnp.concatenate([v, jnp.zeros((count, TILES * LANES - WIDTH), jnp.float32)], axis=1)
+            return pltpu.roll(v, shift, 1)
+
+        before = turned(TILES - 1)
         for c in range(TILES):
-            if c < TILES - 2:
-                v = stage[pl.ds(r, count), c * LANES:(c + 1) * LANES].astype(jnp.float32)
-            elif c == TILES - 2:
-                v = stage[pl.ds(r, count), c * LANES:WIDTH].astype(jnp.float32)
-                v = jnp.concatenate([v, jnp.zeros((count, TILES * LANES - LANES - WIDTH), jnp.float32)], axis=1)
-            now = pltpu.roll(v, shift, 1) if c < TILES - 1 else jnp.zeros((count, LANES), jnp.float32)
+            now = turned(c)
             block = jnp.where(take, now, before)
             if count < LANES:
                 block = jnp.concatenate([block, jnp.zeros((LANES - count, LANES), jnp.float32)], axis=0)
@@ -167,19 +188,13 @@
     prepare(ROWS // LANES * LANES, ROWS % LANES)
 
     def arrived(p):
-        for n, cond in ((TILES - 1, short), (TILES, jnp.logical_not(short))):
-            def some(count, n=n):
-                part = amps.at[pl.ds(0, n * count)]
-                remote(part, part, send_s.at[0, 0], recv.at[p], mate).wait_recv()
-
-            @pl.when(jnp.logical_and(cond, phase_me == p))
-            def _(n=n, some=some):
-                own_copy(n).wait()
-                some(63)
-
-            @pl.when(jnp.logical_and(cond, phase_me != p))
-            def _(some=some):
-                some(64)
+        for cond, count in ((phase_me == p, 63), (phase_me != p, 64)):
+            @pl.when(cond)
+            def _(count=count):
+                part = amps.at[pl.ds(0, TILES * count)]
+                remote(part, part, send_s.at[0], recv.at[p], mate).wait_recv()
+                if count == 63:
+                    own_copy(straight(me)).wait()
 
     def multiply(p):
         arrived(p)
@@ -277,15 +292,8 @@
     @pl.when(k == 0)
     def _():
         sent(0)
-        for q in range(2):
-            @pl.when(parity == q)
-            def _(q=q):
-                if WAITS[q] == 0:
-                    signal(mate)
-                    sent(1)
-                else:
-                    sent(1)
-                    signal(mate)
+        signal(mate)
+        sent(1)
 
     @pl.when(k == 1)
     def _():
@@ -365,6 +373,7 @@
         out_specs=pl.BlockSpec(memory_space=pltpu.VMEM),
         scratch_shapes=[
             pltpu.VMEM((PHASES, TILES, SOURCES, 2, LANES), jnp.bfloat16),
+            pltpu.VMEM((8, 16, TILES + 1, 2, LANES), jnp.bfloat16),
             pltpu.VMEM((ROWS, WIDTH), jnp.bfloat16),
             pltpu.VMEM((TILES * LANES, WIDE), jnp.bfloat16),
             pltpu.VMEM((PHASES, 128, WIDE), jnp.float32),
@@ -379,7 +388,7 @@
             pltpu.VMEM((PHASES, 4, 8, WIDE - CUTS[0][1]), jnp.float32),
             pltpu.VMEM((PHASES * 4, 2, WIDE), jnp.float32),
             pltpu.VMEM((8, 2, WIDE), jnp.float32),
-            dma((2, 2)), dma((PHASES,)), pltpu.SemaphoreType.REGULAR, dma, dma,
+            dma((2,)), dma((PHASES,)), pltpu.SemaphoreType.REGULAR, dma, dma, dma,
             dma, dma((PHASES, 2)), dma, dma((PHASES,)), dma, dma((PHASES,)), dma, dma((PHASES,)), dma, dma((PHASES,)), dma, dma,
         ],
         compiler_params=pltpu.CompilerParams(collective_id=1, has_side_effects=True, vmem_limit_bytes=60 << 20),

time: 95.3 us -> 93.8 us (0.984)
  Pallas kernels: 93.8 us -> 92.2 us
    pallas_call x1, Pallas kernels: 93.8 us -> 92.2 us  [shards(): pl.pallas_call(kernel, out_shape=jax.ShapeDtypeStruct((2, 2, 800), jnp.fl...]
where the time goes in v4:
time: 93.8 us; the launch traced here: 93.5 us
  Pallas kernels  92.2 us (98%)
  local copies, waits for them, and re-layouts  1.31 us (1%)
    pallas_call x1, Pallas kernels, shards(): pl.pallas_call(kernel, out_shape=jax.ShapeDtypeStruct((2, 2, 800), jnp.fl...  92.2 us

profile of v4, /device:TPU:3, one launch (start us, length us, event | category | flops | bytes accessed | tf_op | source)
XLA Modules:
  0.0 93.5 jit_solution(15473398467477804073)
XLA Ops:
  0.0 92.2 %ladder.1 = f32[2,2,800]{2,1,0:T(2,128)} custom-call(bf16[5000,2,128]{2,1,0:T(2,128)(2,1)} %bitcast.5, bf16[1600,2500]{1,0:T(8,128)(2,1)} %bitcast.4), custom_call_target="tpu_custom_call" | custom-call | tf_op jit(solution)/shard_map/ladder/pallas_call | solution.py:369
  92.2 1.3 %copy.4 = f32[2,2,800]{2,1,0:T(2,128)} copy(f32[2,2,800]{2,1,0:T(2,128)} %ladder.1) | data formatting | bytes 25600
